TPU v7x, 512 devices: a whole 4x8x8 slice. The times are simulated.
512 devices in a mesh: gx: 16 (over x, y_hi, core), gy: 32 (over y_lo, z).
Axes of the slice: x: 4, y: 8 (y_hi: 2, y_lo: 4; y = y_hi * 4 + y_lo), z: 8, core: 2. Of those that a mesh axis runs over, the one named last changes fastest.
Arguments:
- bond_mask: int32 [3, 256, 512, 128], P(None, 'gx', 'gy'), may hold values 0 or 1
- levels: float32 [2, 3], replicated, may hold values from 0.3 to 3
- electrode: int32 [2, 256, 512], P(None, 'gx', 'gy'), may hold values 0 or 1
- leakage: float32 [256, 512, 128], P('gx', 'gy'), may hold values from 0.05 to 0.5
- source: float32 [256, 512, 128], P('gx', 'gy'), may hold values from -72 to 72
- weight: float32 [256, 512, 128], P('gx', 'gy'), may hold values from -72 to 72
Outputs:
- potential: float32 [256, 512, 128], P('gx', 'gy')
- adjoint: float32 [256, 512, 128], P('gx', 'gy')
- sensitivity: float32 [3, 256, 512, 128], P(None, 'gx', 'gy')
All inputs are finite; a program needn't handle non-finite values. No bound on the sum of `bond_mask` or of `electrode` on one device may be relied on, other than what follows from the above.
Results may differ from a plain program's by a relative error of at most 0.0003.
Values sent between devices are 32-bit elements; how exact they have to be, the bound alone decides.
No kernel may reach another device: no remote copies, remote signals or barrier semaphores. Data moves between devices by JAX's collectives and lax.ppermute only.
A program may use at most 64 MiB of HBM per device.

v0:
```python
import jax
import jax.numpy as jnp
from jax import lax
from jax.sharding import PartitionSpec as P

ITERS = 4


def extended(block, sides, width):
    for axis, dim in sides:
        count = lax.axis_size(axis)
        forward = [(i, i + 1) for i in range(count - 1)]
        backward = [(target, source) for source, target in forward]
        low = lax.ppermute(
            lax.slice_in_dim(block, block.shape[dim] - width, None, axis=dim), axis, forward
        )
        high = lax.ppermute(lax.slice_in_dim(block, 0, width, axis=dim), axis, backward)
        block = jnp.concatenate([low, block, high], axis=dim)
    return block


def passed_along(value, axis, steps):
    count = lax.axis_size(axis)
    first, last = (max(0, -steps), min(count, count - steps))
    return lax.ppermute(value, axis, [(source, source + steps) for source in range(first, last)])


def totals(left, right):
    return jnp.sum(left * right, axis=(1, 2, 3))


def operate(fields, cond, below, diag):
    padded = extended(fields, (("gx", 1), ("gy", 2)), 1)
    up_x = padded[:, 2:, 1:-1]
    dn_x = padded[:, :-2, 1:-1]
    up_y = padded[:, 1:-1, 2:]
    dn_y = padded[:, 1:-1, :-2]
    zero_plane = jnp.zeros(fields.shape[:3] + (1,), jnp.float32)
    up_z = jnp.concatenate([fields[..., 1:], zero_plane], axis=3)
    dn_z = jnp.concatenate([zero_plane, fields[..., :-1]], axis=3)
    beside = (
        cond[0] * up_x
        + below[0] * dn_x
        + cond[1] * up_y
        + below[1] * dn_y
        + cond[2] * up_z
        + below[2] * dn_z
    )
    return diag * fields - beside


def precond_total(resid, scaled):
    return lax.psum(totals(resid, scaled), ("gx", "gy"))


def solve(rhs, cond, below, diag):
    solution = jnp.zeros_like(rhs)
    resid = rhs
    scaled = resid / diag
    direction = scaled
    norm_now = precond_total(resid, scaled)
    for step in range(ITERS):
        image = operate(direction, cond, below, diag)
        curv = lax.psum(totals(direction, image), ("gx", "gy"))
        alpha = (norm_now / curv)[:, None, None, None]
        solution = solution + alpha * direction
        resid = resid - alpha * image
        if step + 1 < ITERS:
            scaled = resid / diag
            fresh = precond_total(resid, scaled)
            direction = scaled + (fresh / norm_now)[:, None, None, None] * direction
            norm_now = fresh
    return solution


def body(bond_mask, levels, electrode, leakage, source, weight):
    cx, cy, nz = leakage.shape
    shape = (cx, cy, nz)
    row_x = lax.axis_index("gx") * cx + lax.broadcasted_iota(jnp.int32, (cx, 1, 1), 0)
    row_y = lax.axis_index("gy") * cy + lax.broadcasted_iota(jnp.int32, (1, cy, 1), 1)
    col_z = lax.broadcasted_iota(jnp.int32, (1, 1, nz), 2)
    inside = jnp.stack(
        [
            jnp.broadcast_to(row_x < cx * lax.axis_size("gx") - 1, shape),
            jnp.broadcast_to(row_y < cy * lax.axis_size("gy") - 1, shape),
            jnp.broadcast_to(col_z < nz - 1, shape),
        ]
    ).astype(jnp.float32)
    cond = (
        jnp.where(bond_mask == 1, levels[1][:, None, None, None], levels[0][:, None, None, None])
        * inside
    )
    rim_x = passed_along(cond[0, -1:], "gx", 1)
    rim_y = passed_along(cond[1, :, -1:], "gy", 1)
    below_x = jnp.concatenate([rim_x, cond[0, :-1]], axis=0)
    below_y = jnp.concatenate([rim_y, cond[1, :, :-1]], axis=1)
    below_z = jnp.concatenate([jnp.zeros((cx, cy, 1), jnp.float32), cond[2, :, :, :-1]], axis=2)
    below = (below_x, below_y, below_z)
    elec = electrode.astype(jnp.float32)
    first = jnp.where(col_z == 0, elec[0][:, :, None], 0.0)
    last = jnp.where(col_z == nz - 1, elec[1][:, :, None], 0.0)
    diag = leakage + first + last + cond[0] + cond[1] + cond[2] + below_x + below_y + below_z
    rhs = jnp.stack([source + first, weight + last])
    fields = jnp.concatenate(
        [solve(rhs[0:1], cond, below, diag), solve(rhs[1:2], cond, below, diag)], axis=0
    )
    next_x = passed_along(fields[:, :1], "gx", -1)
    next_y = passed_along(fields[:, :, :1], "gy", -1)
    up_x = jnp.concatenate([fields[:, 1:], next_x], axis=1)
    up_y = jnp.concatenate([fields[:, :, 1:], next_y], axis=2)
    up_z = jnp.concatenate([fields[..., 1:], jnp.zeros((2, cx, cy, 1), jnp.float32)], axis=3)
    potential = fields[0]
    adjoint = fields[1]
    sens = jnp.stack(
        [
            -(adjoint - ups[1]) * (potential - ups[0]) * inside[d]
            for d, ups in enumerate((up_x, up_y, up_z))
        ]
    )
    return (potential, adjoint, sens)


def solution(mesh):
    return jax.shard_map(
        body,
        mesh=mesh,
        in_specs=(
            P(None, "gx", "gy", None),
            P(),
            P(None, "gx", "gy"),
            P("gx", "gy", None),
            P("gx", "gy", None),
            P("gx", "gy", None),
        ),
        out_specs=(P("gx", "gy", None), P("gx", "gy", None), P(None, "gx", "gy", None)),
        check_vma=False,
    )
```

profile of v0, /device:TPU:1, one launch (start us, length us, event | category | flops | bytes accessed | tf_op | source)
XLA Modules:
  0.0 1077.7 jit_solution(148761444872244542)
XLA Ops:
  1.5 1.1 select_select_fusion
  2.7 8.8 collective-permute-start
  11.6 4.0 collective-permute-start.1
  16.6 0.8 multiply_reduce_fusion.13
  18.3 3.8 collective-permute-start.19
  22.2 1.9 collective-permute-start.18
  24.2 7.5 collective-permute-start.3
  31.7 1.9 collective-permute-start.2
  33.7 1.3 collective-permute-start.20
  35.0 4.6 collective-permute-start.21
  39.7 1.0 collective-permute-done.2
  40.6 1.3 collective-permute-start.4
  41.9 4.6 collective-permute-start.5
  46.6 0.8 multiply_reduce_fusion.5
  47.4 108.5 %all-reduce.23 = (f32[1]{0:T(128)}, f32[1]{0:T(128)}) all-reduce(f32[1]{0:T(128)} %bitcast.37, f32[1]{0:T(128)} %bitcast.40), channel_id=1, replica_groups=mesh['gx'=16,'gy'=32] {'gx','gy'}, use_global_device_ids=true, to_apply=%region_17.18 | all-reduce | flops 2 | bytes 16 | tf_op jit(solution)/shard_map/psum | solution.py:53
  157.2 0.8 multiply_reduce_fusion.4
  158.0 93.5 %psum.122 = f32[1]{0:T(128)} all-reduce(f32[1]{0:T(128)} %bitcast.44), channel_id=1, replica_groups=mesh['gx'=16,'gy'=32] {'gx','gy'}, use_global_device_ids=true, to_apply=%region_21.22 | all-reduce | flops 1 | bytes 8 | tf_op jit(solution)/shard_map/psum | solution.py:53
  252.9 6.1 collective-permute-start.23
  259.0 1.9 collective-permute-start.22
  261.0 0.8 multiply_reduce_fusion.12
  261.8 6.1 collective-permute-done.22
  267.9 1.3 collective-permute-start.24
  269.2 4.0 collective-permute-start.25
  274.0 0.8 multiply_reduce_fusion.3
  274.8 98.8 %all-reduce.22 = (f32[1]{0:T(128)}, f32[1]{0:T(128)}, f32[1]{0:T(128)}) all-reduce(f32[1]{0:T(128)} %bitcast.47, f32[1]{0:T(128)} %bitcast.12, f32[1]{0:T(128)} %bitcast.18), channel_id=1, replica_groups=mesh['gx'=16,'gy'=32] {'gx','gy'}, use_global_device_ids=true, to_apply=%region_23.24 | all-reduce | flops 3 | bytes 24 | tf_op jit(solution)/shard_map/psum | solution.py:64
  376.2 0.7 multiply_reduce_fusion.2
  377.0 95.3 %all-reduce.21 = (f32[1]{0:T(128)}, f32[1]{0:T(128)}) all-reduce(f32[1]{0:T(128)} %bitcast.23, f32[1]{0:T(128)} %bitcast.49), channel_id=1, replica_groups=mesh['gx'=16,'gy'=32] {'gx','gy'}, use_global_device_ids=true, to_apply=%region_5.6 | all-reduce | flops 2 | bytes 16 | tf_op jit(solution)/shard_map/psum | solution.py:53
  475.0 5.3 collective-permute-start.27
  480.4 1.9 collective-permute-start.26
  482.4 7.5 collective-permute-start.7
  490.0 1.9 collective-permute-start.6
  491.9 1.3 collective-permute-start.28
  493.2 4.0 collective-permute-start.29
  497.2 1.6 collective-permute-done.6
  498.9 1.3 collective-permute-start.8
  500.2 4.0 collective-permute-start.9
  504.2 0.8 multiply_reduce_fusion.1
  504.9 0.8 multiply_reduce_fusion.10
  505.7 104.2 %all-reduce.20 = (f32[1]{0:T(128)}, f32[1]{0:T(128)}) all-reduce(f32[1]{0:T(128)} %bitcast.51, f32[1]{0:T(128)} %bitcast.26), channel_id=1, replica_groups=mesh['gx'=16,'gy'=32] {'gx','gy'}, use_global_device_ids=true, to_apply=%region_27.28 | all-reduce | flops 2 | bytes 16 | tf_op jit(solution)/shard_map/psum | solution.py:64
  613.2 93.5 %psum.116 = f32[1]{0:T(128)} all-reduce(f32[1]{0:T(128)} %bitcast.28), channel_id=1, replica_groups=mesh['gx'=16,'gy'=32] {'gx','gy'}, use_global_device_ids=true, to_apply=%region_9.10 | all-reduce | flops 1 | bytes 8 | tf_op jit(solution)/shard_map/psum | solution.py:53
  708.2 6.5 collective-permute-start.11
  714.7 1.9 collective-permute-start.10
  716.7 6.9 collective-permute-done.10
  723.6 1.3 collective-permute-start.12
  724.9 4.0 collective-permute-start.13
  729.7 0.8 multiply_reduce_fusion.8
  730.6 98.3 %psum.117 = f32[1]{0:T(128)} all-reduce(f32[1]{0:T(128)} %bitcast.30), channel_id=1, replica_groups=mesh['gx'=16,'gy'=32] {'gx','gy'}, use_global_device_ids=true, to_apply=%region_11.12 | all-reduce | flops 1 | bytes 8 | tf_op jit(solution)/shard_map/psum | solution.py:64
  830.9 95.1 %all-reduce.19 = (f32[1]{0:T(128)}, f32[1]{0:T(128)}) all-reduce(f32[1]{0:T(128)} %bitcast.32, f32[1]{0:T(128)} %bitcast.53), channel_id=1, replica_groups=mesh['gx'=16,'gy'=32] {'gx','gy'}, use_global_device_ids=true, to_apply=%region_13.14 | all-reduce | flops 2 | bytes 16 | tf_op jit(solution)/shard_map/psum | solution.py:53
  928.7 5.4 collective-permute-start.31
  934.1 1.9 collective-permute-start.30
  936.2 7.5 collective-permute-start.15
  943.7 1.9 collective-permute-start.14
  945.7 1.3 collective-permute-start.32
  947.0 4.0 collective-permute-start.33
  951.0 1.6 collective-permute-done.14
  952.6 1.3 collective-permute-start.16
  953.9 4.0 collective-permute-start.17
  957.9 0.8 fusion.28
  958.7 0.7 fusion.70
  959.5 104.1 %all-reduce.18 = (f32[1]{0:T(128)}, f32[1]{0:T(128)}) all-reduce(f32[1]{0:T(128)} %bitcast.34, f32[1]{0:T(128)} %bitcast.55), channel_id=1, replica_groups=mesh['gx'=16,'gy'=32] {'gx','gy'}, use_global_device_ids=true, to_apply=%region_15.16 | all-reduce | flops 2 | bytes 16 | tf_op jit(solution)/shard_map/psum | solution.py:64
  1066.5 1.3 collective-permute-start.35
  1067.8 2.6 collective-permute-start.34
  1071.0 5.8 collective-permute-done.34
  1076.9 0.8 pad_maximum_fusion
  (99 shorter events, 7.5 us)
Async XLA Ops:
  0.7 0.7 copy-start.6
  2.7 13.6 %collective-permute-start = (f32[1,16,128]{2,1,0:T(8,128)S(1)}, f32[1,16,128]{2,1,0:T(8,128)S(1)}, u32[]{:S(2)}, u32[]{:S(2)}) collective-permute-start(f32[1,16,128]{2,1,0:T(8,128)S(1)} %slice_bitcast_fusion.4), channel_id=1, source_target_pairs={{0,32},{32,64},{64,96},{96,128},{128,160},{160,192},{192,224},{224... | collective-permute-start | bytes 24584 | tf_op jit(solution)/shard_map/ppermute | solution.py:25
  11.6 4.8 collective-permute-start.1
  15.6 0.7 copy-start.5
  15.6 0.9 copy-start.3
  15.6 1.0 copy-start.4
  16.6 0.9 copy-start.2
  18.3 15.4 %collective-permute-start.19 = (f32[1,1,16,128]{3,2,1,0:T(8,128)S(1)}, f32[1,1,16,128]{3,2,1,0:T(8,128)S(1)}, u32[]{:S(2)}, u32[]{:S(2)}) collective-permute-start(f32[1,1,16,128]{3,2,1,0:T(8,128)S(1)} %get-tuple-element.89), channel_id=1, source_target_pairs={{0,32},{32,64},{64,96},{96,128},{128,160},{160,192},{192,224},{224... | collective-permute-start | bytes 24584 | tf_op jit(solution)/shard_map/ppermute | solution.py:14
  22.2 11.5 %collective-permute-start.18 = (f32[1,1,16,128]{3,2,1,0:T(8,128)S(1)}, f32[1,1,16,128]{3,2,1,0:T(8,128)S(1)}, u32[]{:S(2)}, u32[]{:S(2)}) collective-permute-start(f32[1,1,16,128]{3,2,1,0:T(8,128)S(1)} %get-tuple-element.90), channel_id=1, source_target_pairs={{32,0},{64,32},{96,64},{128,96},{160,128},{192,160},{224,192},{256... | collective-permute-start | bytes 24584 | tf_op jit(solution)/shard_map/ppermute | solution.py:17
  24.2 15.5 %collective-permute-start.3 = (f32[1,1,16,128]{3,2,1,0:T(8,128)S(1)}, f32[1,1,16,128]{3,2,1,0:T(8,128)S(1)}, u32[]{:S(2)}, u32[]{:S(2)}) collective-permute-start(f32[1,1,16,128]{3,2,1,0:T(8,128)S(1)} %get-tuple-element.93), channel_id=1, source_target_pairs={{0,32},{32,64},{64,96},{96,128},{128,160},{160,192},{192,224},{224... | collective-permute-start | bytes 24584 | tf_op jit(solution)/shard_map/ppermute | solution.py:14
  31.7 8.9 collective-permute-start.2
  33.7 12.9 %collective-permute-start.20 = (f32[1,18,1,128]{3,2,1,0:T(1,128)S(1)}, f32[1,18,1,128]{3,2,1,0:T(1,128)S(1)}, u32[]{:S(2)}, u32[]{:S(2)}) collective-permute-start(f32[1,18,1,128]{3,2,1,0:T(1,128)S(1)} %get-tuple-element.57), channel_id=1, source_target_pairs={{1,0},{2,1},{3,2},{4,3},{5,4},{6,5},{7,6},{8,7},{9,8},{10,9},{11,1... | collective-permute-start | bytes 27656 | tf_op jit(solution)/shard_map/ppermute | solution.py:17
  35.0 11.6 %collective-permute-start.21 = (f32[1,18,1,128]{3,2,1,0:T(1,128)S(1)}, f32[1,18,1,128]{3,2,1,0:T(1,128)S(1)}, u32[]{:S(2)}, u32[]{:S(2)}) collective-permute-start(f32[1,18,1,128]{3,2,1,0:T(1,128)S(1)} %get-tuple-element.58), channel_id=1, source_target_pairs={{0,1},{1,2},{2,3},{3,4},{4,5},{5,6},{6,7},{7,8},{8,9},{9,10},{10,1... | collective-permute-start | bytes 27656 | tf_op jit(solution)/shard_map/ppermute | solution.py:14
  40.6 220.3 %collective-permute-start.4 = (f32[1,18,1,128]{3,2,1,0:T(1,128)S(1)}, f32[1,18,1,128]{3,2,1,0:T(1,128)S(1)}, u32[]{:S(2)}, u32[]{:S(2)}) collective-permute-start(f32[1,18,1,128]{3,2,1,0:T(1,128)S(1)} %get-tuple-element.59), channel_id=1, source_target_pairs={{1,0},{2,1},{3,2},{4,3},{5,4},{6,5},{7,6},{8,7},{9,8},{10,9},{11,1... | collective-permute-start | bytes 27656 | tf_op jit(solution)/shard_map/ppermute | solution.py:17
  41.9 219.0 %collective-permute-start.5 = (f32[1,18,1,128]{3,2,1,0:T(1,128)S(1)}, f32[1,18,1,128]{3,2,1,0:T(1,128)S(1)}, u32[]{:S(2)}, u32[]{:S(2)}) collective-permute-start(f32[1,18,1,128]{3,2,1,0:T(1,128)S(1)} %get-tuple-element.60), channel_id=1, source_target_pairs={{0,1},{1,2},{2,3},{3,4},{4,5},{5,6},{6,7},{7,8},{8,9},{9,10},{10,1... | collective-permute-start | bytes 27656 | tf_op jit(solution)/shard_map/ppermute | solution.py:14
  252.9 8.9 collective-permute-start.23
  259.0 8.9 collective-permute-start.22
  267.9 5.4 collective-permute-start.24
  269.2 4.8 collective-permute-start.25
  475.0 16.9 %collective-permute-start.27 = (f32[1,1,16,128]{3,2,1,0:T(8,128)S(1)}, f32[1,1,16,128]{3,2,1,0:T(8,128)S(1)}, u32[]{:S(2)}, u32[]{:S(2)}) collective-permute-start(f32[1,1,16,128]{3,2,1,0:T(8,128)S(1)} %get-tuple-element.79), channel_id=1, source_target_pairs={{0,32},{32,64},{64,96},{96,128},{128,160},{160,192},{192,224},{224... | collective-permute-start | bytes 24584 | tf_op jit(solution)/shard_map/ppermute | solution.py:14
  480.4 11.5 %collective-permute-start.26 = (f32[1,1,16,128]{3,2,1,0:T(8,128)S(1)}, f32[1,1,16,128]{3,2,1,0:T(8,128)S(1)}, u32[]{:S(2)}, u32[]{:S(2)}) collective-permute-start(f32[1,1,16,128]{3,2,1,0:T(8,128)S(1)} %get-tuple-element.80), channel_id=1, source_target_pairs={{32,0},{64,32},{96,64},{128,96},{160,128},{192,160},{224,192},{256... | collective-permute-start | bytes 24584 | tf_op jit(solution)/shard_map/ppermute | solution.py:17
  482.4 14.8 %collective-permute-start.7 = (f32[1,1,16,128]{3,2,1,0:T(8,128)S(1)}, f32[1,1,16,128]{3,2,1,0:T(8,128)S(1)}, u32[]{:S(2)}, u32[]{:S(2)}) collective-permute-start(f32[1,1,16,128]{3,2,1,0:T(8,128)S(1)} %get-tuple-element.75), channel_id=1, source_target_pairs={{0,32},{32,64},{64,96},{96,128},{128,160},{160,192},{192,224},{224... | collective-permute-start | bytes 24584 | tf_op jit(solution)/shard_map/ppermute | solution.py:14
  490.0 8.9 collective-permute-start.6
  491.9 12.2 %collective-permute-start.28 = (f32[1,18,1,128]{3,2,1,0:T(1,128)S(1)}, f32[1,18,1,128]{3,2,1,0:T(1,128)S(1)}, u32[]{:S(2)}, u32[]{:S(2)}) collective-permute-start(f32[1,18,1,128]{3,2,1,0:T(1,128)S(1)} %get-tuple-element.53), channel_id=1, source_target_pairs={{1,0},{2,1},{3,2},{4,3},{5,4},{6,5},{7,6},{8,7},{9,8},{10,9},{11,1... | collective-permute-start | bytes 27656 | tf_op jit(solution)/shard_map/ppermute | solution.py:17
  493.2 10.9 %collective-permute-start.29 = (f32[1,18,1,128]{3,2,1,0:T(1,128)S(1)}, f32[1,18,1,128]{3,2,1,0:T(1,128)S(1)}, u32[]{:S(2)}, u32[]{:S(2)}) collective-permute-start(f32[1,18,1,128]{3,2,1,0:T(1,128)S(1)} %get-tuple-element.54), channel_id=1, source_target_pairs={{0,1},{1,2},{2,3},{3,4},{4,5},{5,6},{6,7},{7,8},{8,9},{9,10},{10,1... | collective-permute-start | bytes 27656 | tf_op jit(solution)/shard_map/ppermute | solution.py:14
  498.9 6.1 collective-permute-start.8
  500.2 4.8 collective-permute-start.9
  708.2 8.5 collective-permute-start.11
  714.7 8.9 collective-permute-start.10
  723.6 5.4 collective-permute-start.12
  724.9 4.8 collective-permute-start.13
  928.7 16.9 %collective-permute-start.31 = (f32[1,1,16,128]{3,2,1,0:T(8,128)S(1)}, f32[1,1,16,128]{3,2,1,0:T(8,128)S(1)}, u32[]{:S(2)}, u32[]{:S(2)}) collective-permute-start(f32[1,1,16,128]{3,2,1,0:T(8,128)S(1)} %get-tuple-element.63), channel_id=1, source_target_pairs={{0,32},{32,64},{64,96},{96,128},{128,160},{160,192},{192,224},{224... | collective-permute-start | bytes 24584 | tf_op jit(solution)/shard_map/ppermute | solution.py:14
  934.1 11.5 %collective-permute-start.30 = (f32[1,1,16,128]{3,2,1,0:T(8,128)S(1)}, f32[1,1,16,128]{3,2,1,0:T(8,128)S(1)}, u32[]{:S(2)}, u32[]{:S(2)}) collective-permute-start(f32[1,1,16,128]{3,2,1,0:T(8,128)S(1)} %get-tuple-element.64), channel_id=1, source_target_pairs={{32,0},{64,32},{96,64},{128,96},{160,128},{192,160},{224,192},{256... | collective-permute-start | bytes 24584 | tf_op jit(solution)/shard_map/ppermute | solution.py:17
  936.2 14.8 %collective-permute-start.15 = (f32[1,1,16,128]{3,2,1,0:T(8,128)S(1)}, f32[1,1,16,128]{3,2,1,0:T(8,128)S(1)}, u32[]{:S(2)}, u32[]{:S(2)}) collective-permute-start(f32[1,1,16,128]{3,2,1,0:T(8,128)S(1)} %get-tuple-element.69), channel_id=1, source_target_pairs={{0,32},{32,64},{64,96},{96,128},{128,160},{160,192},{192,224},{224... | collective-permute-start | bytes 24584 | tf_op jit(solution)/shard_map/ppermute | solution.py:14
  943.7 8.9 collective-permute-start.14
  945.7 12.2 %collective-permute-start.32 = (f32[1,18,1,128]{3,2,1,0:T(1,128)S(1)}, f32[1,18,1,128]{3,2,1,0:T(1,128)S(1)}, u32[]{:S(2)}, u32[]{:S(2)}) collective-permute-start(f32[1,18,1,128]{3,2,1,0:T(1,128)S(1)} %get-tuple-element.45), channel_id=1, source_target_pairs={{1,0},{2,1},{3,2},{4,3},{5,4},{6,5},{7,6},{8,7},{9,8},{10,9},{11,1... | collective-permute-start | bytes 27656 | tf_op jit(solution)/shard_map/ppermute | solution.py:17
  947.0 10.9 %collective-permute-start.33 = (f32[1,18,1,128]{3,2,1,0:T(1,128)S(1)}, f32[1,18,1,128]{3,2,1,0:T(1,128)S(1)}, u32[]{:S(2)}, u32[]{:S(2)}) collective-permute-start(f32[1,18,1,128]{3,2,1,0:T(1,128)S(1)} %get-tuple-element.46), channel_id=1, source_target_pairs={{0,1},{1,2},{2,3},{3,4},{4,5},{5,6},{6,7},{7,8},{8,9},{9,10},{10,1... | collective-permute-start | bytes 27656 | tf_op jit(solution)/shard_map/ppermute | solution.py:14
  952.6 6.1 collective-permute-start.16
  953.9 4.8 collective-permute-start.17
  1066.2 10.6 copy-start
  1066.3 10.5 copy-start.1
  1066.5 4.5 collective-permute-start.35
  1067.8 9.0 collective-permute-start.34
where the time goes:
time: 1080 us
  blocking collectives  891 us (82%)
  starting transfers between devices  125 us (12%)
  waiting for transfers between devices  25 us (2%)
  between operations  19.9 us (2%)
  other arithmetic  13.4 us (1%)
    psum x5, blocking collectives, precond_total(): return lax.psum(totals(resid, scaled), ('gx', 'gy'))  486 us
    psum x4, blocking collectives, solve(): curv = lax.psum(totals(direction, image), ('gx', 'gy'))  405 us
    ppermute x16, starting transfers between devices, extended(): lax.ppermute(lax.slice_in_dim(block, block.shape[dim] - width, None, axis...  83 us
    ppermute x16, starting transfers between devices, extended(): lax.ppermute(lax.slice_in_dim(block, 0, width, axis=dim), axis, backward)  25.7 us
  transfers between devices with their start and end apart: 36, of which 9 were waited for; matrix products, arithmetic and copies ran while one was open for 0% of the time, Pallas kernels for 0%

commit v1 on v0

--- a/solution.py
+++ b/solution.py
@@ -4,6 +4,11 @@
 from jax.sharding import PartitionSpec as P
 
 ITERS = 4
+
+
+def by_each_axis(x, one, other):
+    half = lax.psum(x, one)
+    return lax.psum(half, other)
 
 
 def extended(block, sides, width):
@@ -61,7 +66,7 @@
     norm_now = precond_total(resid, scaled)
     for step in range(ITERS):
         image = operate(direction, cond, below, diag)
-        curv = lax.psum(totals(direction, image), ("gx", "gy"))
+        curv = by_each_axis(totals(direction, image), "gy", "gx")
         alpha = (norm_now / curv)[:, None, None, None]
         solution = solution + alpha * direction
         resid = resid - alpha * image

time: 1080 us -> 1260 us (1.17)
  blocking collectives: 891 us -> 1080 us
    psum x4 -> x10, blocking collectives: 405 us -> 595 us  [the longest x5 319 us: by_each_axis(): half = lax.psum(x, one)]
  transfers between devices with their start and end apart: 36 -> 36, of which waited for: 9 -> 8; matrix products, arithmetic and copies ran while one was open for 0% -> 0% of each run, Pallas kernels for 0% -> 0%
where the time goes in v1:
time: 1260 us; the launch traced here: 1250 us
  blocking collectives  1080 us (86%)
  starting transfers between devices  117 us (9%)
  waiting for transfers between devices  24.6 us (2%)
  between operations  19.4 us (2%)
  other arithmetic  13.2 us (1%)
    psum x5, blocking collectives, precond_total(): return lax.psum(totals(resid, scaled), ('gx', 'gy'))  481 us
    psum x5, blocking collectives, by_each_axis(): half = lax.psum(x, one)  319 us
    psum x5, blocking collectives, by_each_axis(): return lax.psum(half, other)  276 us
    ppermute x16, starting transfers between devices, extended(): lax.ppermute(lax.slice_in_dim(block, block.shape[dim] - width, None, axis...  74.8 us
    ppermute x16, starting transfers between devices, extended(): lax.ppermute(lax.slice_in_dim(block, 0, width, axis=dim), axis, backward)  25.7 us
  transfers between devices with their start and end apart: 36, of which 8 were waited for; matrix products, arithmetic and copies ran while one was open for 0% of the time, Pallas kernels for 0%

profile of v1, /device:TPU:1, one launch (start us, length us, event | category | flops | bytes accessed | tf_op | source)
XLA Modules:
  0.0 1253.1 jit_solution(7940689306928079018)
XLA Ops:
  1.5 1.1 select_select_fusion
  2.7 8.8 collective-permute-start
  11.6 4.0 collective-permute-start.1
  16.6 0.8 multiply_reduce_fusion.13
  18.3 3.8 collective-permute-start.19
  22.2 1.9 collective-permute-start.18
  24.2 7.5 collective-permute-start.3
  31.7 1.9 collective-permute-start.2
  33.7 105.4 %psum.180 = f32[1]{0:T(128)} all-reduce(f32[1]{0:T(128)} %bitcast.37), channel_id=1, replica_groups=mesh['gx'=16,'gy'=32] {'gx','gy'}, use_global_device_ids=true, to_apply=%region_21.22 | all-reduce | flops 1 | bytes 8 | tf_op jit(solution)/shard_map/psum | solution.py:58
  139.1 1.3 collective-permute-start.20
  140.4 4.0 collective-permute-start.21
  144.4 1.3 collective-permute-start.4
  145.7 0.8 multiply_reduce_fusion.5
  146.5 65.1 %psum.181 = f32[1]{0:T(128)} all-reduce(f32[1]{0:T(128)} %bitcast.40), channel_id=1, replica_groups=mesh['gx'=16,'gy'=32] {'gy'}, use_global_device_ids=true, to_apply=%region_23.24 | all-reduce | flops 1 | bytes 8 | tf_op jit(solution)/shard_map/psum | solution.py:10
  211.6 1.3 collective-permute-start.5
  212.9 58.0 %psum.182 = f32[1]{0:T(128)} all-reduce(f32[1]{0:T(128)} %psum.181), channel_id=1, replica_groups=mesh['gx'=16,'gy'=32] {'gx'}, use_global_device_ids=true, to_apply=%region_24.25 | all-reduce | flops 1 | bytes 8 | tf_op jit(solution)/shard_map/psum | solution.py:11
  272.9 93.6 %all-reduce.20 = (f32[1]{0:T(128)}, f32[1]{0:T(128)}) all-reduce(f32[1]{0:T(128)} %bitcast.44, f32[1]{0:T(128)} %bitcast.12), channel_id=1, replica_groups=mesh['gx'=16,'gy'=32] {'gx','gy'}, use_global_device_ids=true, to_apply=%region_26.27 | all-reduce | flops 2 | bytes 16 | tf_op jit(solution)/shard_map/psum | solution.py:58
  367.9 4.6 collective-permute-start.23
  372.5 1.9 collective-permute-start.22
  374.5 0.8 multiply_reduce_fusion.12
  375.2 6.1 collective-permute-done.22
  381.4 1.3 collective-permute-start.24
  382.7 4.0 collective-permute-start.25
  387.5 0.8 multiply_reduce_fusion.3
  388.3 63.7 %all-reduce.23 = (f32[1]{0:T(128)}, f32[1]{0:T(128)}) all-reduce(f32[1]{0:T(128)} %bitcast.47, f32[1]{0:T(128)} %bitcast.18), channel_id=1, replica_groups=mesh['gx'=16,'gy'=32] {'gy'}, use_global_device_ids=true, to_apply=%region_28.29 | all-reduce | flops 2 | bytes 16 | tf_op jit(solution)/shard_map/psum | solution.py:10
  452.0 52.3 %all-reduce.26 = (f32[1]{0:T(128)}, f32[1]{0:T(128)}) all-reduce(f32[1]{0:T(128)} %get-tuple-element.17, f32[1]{0:T(128)} %get-tuple-element.18), channel_id=1, replica_groups=mesh['gx'=16,'gy'=32] {'gx'}, use_global_device_ids=true, to_apply=%region_29.30 | all-reduce | flops 2 | bytes 16 | tf_op jit(solution)/shard_map/psum | solution.py:11
  507.7 94.1 %all-reduce.19 = (f32[1]{0:T(128)}, f32[1]{0:T(128)}) all-reduce(f32[1]{0:T(128)} %bitcast.23, f32[1]{0:T(128)} %bitcast.49), channel_id=1, replica_groups=mesh['gx'=16,'gy'=32] {'gx','gy'}, use_global_device_ids=true, to_apply=%region_6.7 | all-reduce | flops 2 | bytes 16 | tf_op jit(solution)/shard_map/psum | solution.py:58
  604.6 4.6 collective-permute-start.27
  609.2 1.9 collective-permute-start.26
  611.2 7.5 collective-permute-start.7
  618.8 1.9 collective-permute-start.6
  620.8 1.3 collective-permute-start.28
  622.1 4.0 collective-permute-start.29
  626.1 1.6 collective-permute-done.6
  627.7 1.3 collective-permute-start.8
  629.0 4.0 collective-permute-start.9
  634.5 63.2 %all-reduce.22 = (f32[1]{0:T(128)}, f32[1]{0:T(128)}) all-reduce(f32[1]{0:T(128)} %bitcast.51, f32[1]{0:T(128)} %bitcast.26), channel_id=1, replica_groups=mesh['gx'=16,'gy'=32] {'gy'}, use_global_device_ids=true, to_apply=%region_33.34 | all-reduce | flops 2 | bytes 16 | tf_op jit(solution)/shard_map/psum | solution.py:10
  697.7 56.8 %all-reduce.25 = (f32[1]{0:T(128)}, f32[1]{0:T(128)}) all-reduce(f32[1]{0:T(128)} %get-tuple-element.15, f32[1]{0:T(128)} %get-tuple-element.16), channel_id=1, replica_groups=mesh['gx'=16,'gy'=32] {'gx'}, use_global_device_ids=true, to_apply=%region_34.35 | all-reduce | flops 2 | bytes 16 | tf_op jit(solution)/shard_map/psum | solution.py:11
  757.9 94.8 %psum.174 = f32[1]{0:T(128)} all-reduce(f32[1]{0:T(128)} %bitcast.28), channel_id=1, replica_groups=mesh['gx'=16,'gy'=32] {'gx','gy'}, use_global_device_ids=true, to_apply=%region_11.12 | all-reduce | flops 1 | bytes 8 | tf_op jit(solution)/shard_map/psum | solution.py:58
  853.9 5.0 collective-permute-start.11
  858.9 1.9 collective-permute-start.10
  860.8 6.9 collective-permute-done.10
  867.8 1.3 collective-permute-start.12
  869.1 4.0 collective-permute-start.13
  873.9 0.8 multiply_reduce_fusion.8
  874.6 63.6 %psum.175 = f32[1]{0:T(128)} all-reduce(f32[1]{0:T(128)} %bitcast.30), channel_id=1, replica_groups=mesh['gx'=16,'gy'=32] {'gy'}, use_global_device_ids=true, to_apply=%region_13.14 | all-reduce | flops 1 | bytes 8 | tf_op jit(solution)/shard_map/psum | solution.py:10
  938.3 52.2 %psum.176 = f32[1]{0:T(128)} all-reduce(f32[1]{0:T(128)} %psum.175), channel_id=1, replica_groups=mesh['gx'=16,'gy'=32] {'gx'}, use_global_device_ids=true, to_apply=%region_14.15 | all-reduce | flops 1 | bytes 8 | tf_op jit(solution)/shard_map/psum | solution.py:11
  992.4 93.6 %all-reduce.18 = (f32[1]{0:T(128)}, f32[1]{0:T(128)}) all-reduce(f32[1]{0:T(128)} %bitcast.32, f32[1]{0:T(128)} %bitcast.53), channel_id=1, replica_groups=mesh['gx'=16,'gy'=32] {'gx','gy'}, use_global_device_ids=true, to_apply=%region_16.17 | all-reduce | flops 2 | bytes 16 | tf_op jit(solution)/shard_map/psum | solution.py:58
  1088.7 5.0 collective-permute-start.31
  1093.7 1.9 collective-permute-start.30
  1095.7 7.5 collective-permute-start.15
  1103.3 1.9 collective-permute-start.14
  1105.3 1.3 collective-permute-start.32
  1106.6 4.0 collective-permute-start.33
  1110.6 1.6 collective-permute-done.14
  1112.2 1.3 collective-permute-start.16
  1113.5 4.0 collective-permute-start.17
  1119.0 63.2 %all-reduce.21 = (f32[1]{0:T(128)}, f32[1]{0:T(128)}) all-reduce(f32[1]{0:T(128)} %bitcast.34, f32[1]{0:T(128)} %bitcast.55), channel_id=1, replica_groups=mesh['gx'=16,'gy'=32] {'gy'}, use_global_device_ids=true, to_apply=%region_18.19 | all-reduce | flops 2 | bytes 16 | tf_op jit(solution)/shard_map/psum | solution.py:10
  1182.2 56.9 %all-reduce.24 = (f32[1]{0:T(128)}, f32[1]{0:T(128)}) all-reduce(f32[1]{0:T(128)} %get-tuple-element.13, f32[1]{0:T(128)} %get-tuple-element.14), channel_id=1, replica_groups=mesh['gx'=16,'gy'=32] {'gx'}, use_global_device_ids=true, to_apply=%region_19.20 | all-reduce | flops 2 | bytes 16 | tf_op jit(solution)/shard_map/psum | solution.py:11
  1241.9 1.3 collective-permute-start.35
  1243.2 2.1 collective-permute-start.34
  1245.3 1.1 collective-permute-done.35
  1246.4 5.8 collective-permute-done.34
  1252.3 0.8 pad_maximum_fusion
  (105 shorter events, 11.5 us)
Async XLA Ops:
  0.7 0.7 copy-start.6
  2.7 13.6 %collective-permute-start = (f32[1,16,128]{2,1,0:T(8,128)S(1)}, f32[1,16,128]{2,1,0:T(8,128)S(1)}, u32[]{:S(2)}, u32[]{:S(2)}) collective-permute-start(f32[1,16,128]{2,1,0:T(8,128)S(1)} %slice_bitcast_fusion.4), channel_id=1, source_target_pairs={{0,32},{32,64},{64,96},{96,128},{128,160},{160,192},{192,224},{224... | collective-permute-start | bytes 24584 | tf_op jit(solution)/shard_map/ppermute | solution.py:30
  11.6 4.8 collective-permute-start.1
  15.6 0.7 copy-start.5
  15.6 0.9 copy-start.3
  15.6 1.0 copy-start.4
  16.6 0.9 copy-start.2
  18.3 120.8 %collective-permute-start.19 = (f32[1,1,16,128]{3,2,1,0:T(8,128)S(1)}, f32[1,1,16,128]{3,2,1,0:T(8,128)S(1)}, u32[]{:S(2)}, u32[]{:S(2)}) collective-permute-start(f32[1,1,16,128]{3,2,1,0:T(8,128)S(1)} %get-tuple-element.94), channel_id=1, source_target_pairs={{0,32},{32,64},{64,96},{96,128},{128,160},{160,192},{192,224},{224... | collective-permute-start | bytes 24584 | tf_op jit(solution)/shard_map/ppermute | solution.py:19
  22.2 116.9 %collective-permute-start.18 = (f32[1,1,16,128]{3,2,1,0:T(8,128)S(1)}, f32[1,1,16,128]{3,2,1,0:T(8,128)S(1)}, u32[]{:S(2)}, u32[]{:S(2)}) collective-permute-start(f32[1,1,16,128]{3,2,1,0:T(8,128)S(1)} %get-tuple-element.95), channel_id=1, source_target_pairs={{32,0},{64,32},{96,64},{128,96},{160,128},{192,160},{224,192},{256... | collective-permute-start | bytes 24584 | tf_op jit(solution)/shard_map/ppermute | solution.py:22
  24.2 120.2 %collective-permute-start.3 = (f32[1,1,16,128]{3,2,1,0:T(8,128)S(1)}, f32[1,1,16,128]{3,2,1,0:T(8,128)S(1)}, u32[]{:S(2)}, u32[]{:S(2)}) collective-permute-start(f32[1,1,16,128]{3,2,1,0:T(8,128)S(1)} %get-tuple-element.98), channel_id=1, source_target_pairs={{0,32},{32,64},{64,96},{96,128},{128,160},{160,192},{192,224},{224... | collective-permute-start | bytes 24584 | tf_op jit(solution)/shard_map/ppermute | solution.py:19
  31.7 112.6 %collective-permute-start.2 = (f32[1,1,16,128]{3,2,1,0:T(8,128)S(1)}, f32[1,1,16,128]{3,2,1,0:T(8,128)S(1)}, u32[]{:S(2)}, u32[]{:S(2)}) collective-permute-start(f32[1,1,16,128]{3,2,1,0:T(8,128)S(1)} %get-tuple-element.99), channel_id=1, source_target_pairs={{32,0},{64,32},{96,64},{128,96},{160,128},{192,160},{224,192},{256... | collective-permute-start | bytes 24584 | tf_op jit(solution)/shard_map/ppermute | solution.py:22
  139.1 6.6 collective-permute-start.20
  140.4 5.4 collective-permute-start.21
  144.4 230.0 %collective-permute-start.4 = (f32[1,18,1,128]{3,2,1,0:T(1,128)S(1)}, f32[1,18,1,128]{3,2,1,0:T(1,128)S(1)}, u32[]{:S(2)}, u32[]{:S(2)}) collective-permute-start(f32[1,18,1,128]{3,2,1,0:T(1,128)S(1)} %get-tuple-element.64), channel_id=1, source_target_pairs={{1,0},{2,1},{3,2},{4,3},{5,4},{6,5},{7,6},{8,7},{9,8},{10,9},{11,1... | collective-permute-start | bytes 27656 | tf_op jit(solution)/shard_map/ppermute | solution.py:22
  211.6 162.9 %collective-permute-start.5 = (f32[1,18,1,128]{3,2,1,0:T(1,128)S(1)}, f32[1,18,1,128]{3,2,1,0:T(1,128)S(1)}, u32[]{:S(2)}, u32[]{:S(2)}) collective-permute-start(f32[1,18,1,128]{3,2,1,0:T(1,128)S(1)} %get-tuple-element.65), channel_id=1, source_target_pairs={{0,1},{1,2},{2,3},{3,4},{4,5},{5,6},{6,7},{7,8},{8,9},{9,10},{10,1... | collective-permute-start | bytes 27656 | tf_op jit(solution)/shard_map/ppermute | solution.py:19
  367.9 7.4 collective-permute-start.23
  372.5 8.9 collective-permute-start.22
  381.4 5.4 collective-permute-start.24
  382.7 4.8 collective-permute-start.25
  604.6 16.1 %collective-permute-start.27 = (f32[1,1,16,128]{3,2,1,0:T(8,128)S(1)}, f32[1,1,16,128]{3,2,1,0:T(8,128)S(1)}, u32[]{:S(2)}, u32[]{:S(2)}) collective-permute-start(f32[1,1,16,128]{3,2,1,0:T(8,128)S(1)} %get-tuple-element.84), channel_id=1, source_target_pairs={{0,32},{32,64},{64,96},{96,128},{128,160},{160,192},{192,224},{224... | collective-permute-start | bytes 24584 | tf_op jit(solution)/shard_map/ppermute | solution.py:19
  609.2 11.5 collective-permute-start.26
  611.2 14.8 %collective-permute-start.7 = (f32[1,1,16,128]{3,2,1,0:T(8,128)S(1)}, f32[1,1,16,128]{3,2,1,0:T(8,128)S(1)}, u32[]{:S(2)}, u32[]{:S(2)}) collective-permute-start(f32[1,1,16,128]{3,2,1,0:T(8,128)S(1)} %get-tuple-element.80), channel_id=1, source_target_pairs={{0,32},{32,64},{64,96},{96,128},{128,160},{160,192},{192,224},{224... | collective-permute-start | bytes 24584 | tf_op jit(solution)/shard_map/ppermute | solution.py:19
  618.8 8.9 collective-permute-start.6
  620.8 12.2 collective-permute-start.28
  622.1 10.9 collective-permute-start.29
  627.7 6.1 collective-permute-start.8
  629.0 4.8 collective-permute-start.9
  853.9 6.9 collective-permute-start.11
  858.9 8.9 collective-permute-start.10
  867.8 5.4 collective-permute-start.12
  869.1 4.8 collective-permute-start.13
  1088.7 16.5 %collective-permute-start.31 = (f32[1,1,16,128]{3,2,1,0:T(8,128)S(1)}, f32[1,1,16,128]{3,2,1,0:T(8,128)S(1)}, u32[]{:S(2)}, u32[]{:S(2)}) collective-permute-start(f32[1,1,16,128]{3,2,1,0:T(8,128)S(1)} %get-tuple-element.68), channel_id=1, source_target_pairs={{0,32},{32,64},{64,96},{96,128},{128,160},{160,192},{192,224},{224... | collective-permute-start | bytes 24584 | tf_op jit(solution)/shard_map/ppermute | solution.py:19
  1093.7 11.5 collective-permute-start.30
  1095.7 14.8 %collective-permute-start.15 = (f32[1,1,16,128]{3,2,1,0:T(8,128)S(1)}, f32[1,1,16,128]{3,2,1,0:T(8,128)S(1)}, u32[]{:S(2)}, u32[]{:S(2)}) collective-permute-start(f32[1,1,16,128]{3,2,1,0:T(8,128)S(1)} %get-tuple-element.74), channel_id=1, source_target_pairs={{0,32},{32,64},{64,96},{96,128},{128,160},{160,192},{192,224},{224... | collective-permute-start | bytes 24584 | tf_op jit(solution)/shard_map/ppermute | solution.py:19
  1103.3 8.9 collective-permute-start.14
  1105.3 12.2 collective-permute-start.32
  1106.6 10.9 collective-permute-start.33
  1112.2 6.1 collective-permute-start.16
  1113.5 4.8 collective-permute-start.17
  1241.6 10.6 copy-start
  1241.7 10.5 copy-start.1
  1241.9 4.5 collective-permute-start.35
  1243.2 9.0 collective-permute-start.34
